TPU v7x, 32 devices: a whole 2x2x4 slice. The times are simulated.
32 devices in a mesh: row: 4 (over y, x), col: 8 (over z, core).
Axes of the slice: x: 2, y: 2, z: 4, core: 2. Of those that a mesh axis runs over, the one named last changes fastest.
Arguments:
- inverses: bfloat16 [4, 32, 1024, 1024], P('row', 'col'), as said below
- coupling: bfloat16 [4, 32, 1024, 256], P('row', 'col'), may hold values from -0.1875 to 0.1875
- orders: int32 [4, 32], P('row', 'col'), may hold values from 512 to 1024, as said below
- owners: int32 [4, 32, 1], P(None, 'col'), may hold values from 0 to 3, as said below
- offsets: int32 [4, 32, 2], P(None, 'col'), may hold values from 0 to 2
- dense_slab: float32 [2048, 4096], P('row', 'col'), may hold values from -6 to 6
- pivots: float32 [1024], replicated, may hold values from 16 to 128
Outputs:
- result: float32 [2048, 4096], P('row', 'col')
Inputs may be any that keep to these rules, and one draw needn't show every extreme that they name: `orders`: order of each subdomain; some subdomain has exactly 1024. `owners`: within the 4 subdomains of one device (entries r, s with the same r and the same s // 4) no row block is named twice. `inverses`: each inverse is symmetric.
All inputs are finite; a program needn't handle non-finite values.
Results may differ from a plain program's by a relative error of at most 0.0035.
Values may be sent and summed in bfloat16 or wider, within the bound.
A program may use at most 64 MiB of HBM per device.

v0:
```python
import jax
import jax.numpy as jnp
from jax import lax
from jax.sharding import PartitionSpec as P

CAP = 1


def spread(value, axis, source):
    kept = jnp.where(lax.axis_index(axis) == source, value, 0).astype(value.dtype)
    return lax.psum(kept, axis)


def place_tile(schur_sum, tile_value, weight, row_start, col_start):
    couple_width = tile_value.shape[0]
    current = lax.dynamic_slice(schur_sum, (row_start, col_start), (couple_width, couple_width))
    return lax.dynamic_update_slice(
        schur_sum, current + weight * tile_value.astype(jnp.float32), (row_start, col_start)
    )


def body(inverses, coupling, orders, owners, offsets, dense_slab, pivots):
    sub_count = inverses.shape[1]
    order_size = inverses.shape[2]
    couple_width = coupling.shape[3]
    tile_size = dense_slab.shape[0]
    panel_width = pivots.shape[0]
    offset_unit = (tile_size - couple_width) // 2
    live_rows = jnp.arange(order_size, dtype=jnp.int32)[None, :, None] < orders[0][:, None, None]
    masked = jnp.where(live_rows, coupling[0], jnp.zeros_like(coupling[0]))
    solved = jnp.einsum(
        "sij,sjk->sik", inverses[0], masked, preferred_element_type=jnp.float32
    ).astype(jnp.bfloat16)
    schur_tiles = jnp.einsum(
        "sji,sjk->sik", masked, solved, preferred_element_type=jnp.float32
    ).astype(jnp.bfloat16)
    my_row = lax.axis_index("row")
    targets = owners[:, :, 0].reshape(-1)
    row_starts = offsets[:, :, 0].reshape(-1) * offset_unit
    col_starts = offsets[:, :, 1].reshape(-1) * offset_unit
    zero_sum = jnp.zeros((tile_size, tile_size), jnp.float32)
    row_count = lax.axis_size("row")
    grouped = targets.reshape(row_count, sub_count)
    same_owner = grouped[:, :, None] == grouped[:, None, :]
    earlier = jnp.arange(sub_count)[None, :] < jnp.arange(sub_count)[:, None]
    slot_rank = jnp.sum((same_owner & earlier[None]).astype(jnp.int32), axis=2).reshape(-1)
    my_targets = lax.dynamic_slice_in_dim(targets, my_row * sub_count, sub_count)
    my_ranks = lax.dynamic_slice_in_dim(slot_rank, my_row * sub_count, sub_count)
    slot_ids = my_targets * CAP + my_ranks
    selector = (slot_ids[:, None] == jnp.arange(row_count * CAP, dtype=jnp.int32)[None, :]).astype(
        jnp.bfloat16
    )
    flat_tiles = schur_tiles.reshape(sub_count, couple_width * couple_width)
    send_slots = jnp.dot(selector.T, flat_tiles, preferred_element_type=jnp.float32).astype(
        jnp.bfloat16
    )
    send_slots = send_slots.reshape(row_count, CAP, couple_width, couple_width)
    received = lax.all_to_all(send_slots, "row", split_axis=0, concat_axis=0, tiled=True)

    def one_slot(position, running):
        source = position // sub_count
        weight = (targets[position] == my_row).astype(jnp.float32)
        tile_value = received[source, jnp.minimum(slot_rank[position], CAP - 1)]
        return place_tile(running, tile_value, weight, row_starts[position], col_starts[position])

    schur_sum = lax.fori_loop(0, targets.shape[0], one_slot, zero_sum)
    updated = dense_slab - schur_sum
    rounded = updated.astype(jnp.bfloat16)
    panel_parts = []
    for part_index in range(panel_width // tile_size):
        panel_parts.append(spread(rounded, "row", part_index))
    panel_cols = jnp.concatenate(panel_parts, axis=0)
    crossed = spread(panel_cols, "col", lax.axis_index("row"))
    left_factor = (crossed.astype(jnp.float32) / pivots[:, None]).astype(jnp.bfloat16)
    update = lax.dot_general(
        left_factor, panel_cols, (((0,), (0,)), ((), ())), preferred_element_type=jnp.float32
    )
    return updated - update


def solution(mesh):
    placed = (
        P("row", "col", None, None),
        P("row", "col", None, None),
        P("row", "col"),
        P(None, "col", None),
        P(None, "col", None),
        P("row", "col"),
        P(),
    )
    return jax.shard_map(
        body, mesh=mesh, in_specs=placed, out_specs=P("row", "col"), check_vma=False
    )
```

profile of v0, /device:TPU:0, one launch (start us, length us, event | category | flops | bytes accessed | tf_op | source)
XLA Modules:
  0.0 317.4 jit_solution(6392637798119528049)
XLA Ops:
  6.5 1.0 convert_reduce_fusion
  8.1 1.3 reduce.11
  9.5 0.7 iota_compare_fusion
  10.3 7.5 %fusion.13 = bf16[1,4,256,256]{3,2,1,0:T(8,128)(2,1)S(1)} fusion(bf16[1,4,1024,1024]{3,2,1,0:T(8,128)(2,1)} %param.9, bf16[1,4,1024,256]{3,2,1,0:T(8,128)(2,1)} %param.10, pred[4,1024]{1,0:T(4,128)(4,1)S(1)} %iota_compare_fusion), kind=kOutput, calls=%fused_computation.10 | convolution fusion | flops 2687762432 | bytes 11014144 | tf_op jit(solution)/shard_map/sji,sjk->sik/dot_general | solution.py:34
  18.9 0.9 copy.20
  19.7 5.2 %all-to-all-start = ((bf16[4,1,256,256]{3,2,1,0:T(8,128)(2,1)}), bf16[4,1,256,256]{3,2,1,0:T(8,128)(2,1)S(1)}, u32[]{:S(2)}, u32[]{:S(2)}) async-start(bf16[4,1,256,256]{3,2,1,0:T(8,128)(2,1)} %bitcast.48), calls=%async_computation | async-start | bytes 1048576 | tf_op jit(solution)/shard_map/all_to_all | solution.py:58
  25.1 7.8 %all-to-all-done = bf16[4,1,256,256]{3,2,1,0:T(8,128)(2,1)S(1)} async-done(((bf16[4,1,256,256]{3,2,1,0:T(8,128)(2,1)}), bf16[4,1,256,256]{3,2,1,0:T(8,128)(2,1)S(1)}, u32[]{:S(2)}, u32[]{:S(2)}) %all-to-all-start) | async-done | bytes 524320 | tf_op jit(solution)/shard_map/all_to_all | solution.py:58
  33.1 157.7 %while.15 = (s32[]{:T(128)}, f32[512,512]{1,0:T(8,128)S(1)}, s32[16]{0:T(128)S(1)}, s32[16]{0:T(128)S(1)}, s32[16]{0:T(128)S(1)}, /*index=5*/s32[]{:T(128)}, bf1...) while((s32[]{:T(128)}, f32[512,512]{1,0:T(8,128)S(1)}, ...), condition=%wide.region_2.3_spmd, body=%wide.region_1.2_spmd.sunk | while | flops 196629 | bytes 1180039 | solution.py:66
  38.2 0.6 dynamic_slice.75
  39.6 2.6 dynamic_update_slice.11
  47.2 0.6 dynamic_slice.75
  48.6 2.6 dynamic_update_slice.11
  56.3 0.6 dynamic_slice.75
  57.7 4.7 %dynamic_update_slice.11 = f32[512,512]{1,0:T(8,128)S(1)} dynamic-update-slice(f32[512,512]{1,0:T(8,128)S(1)} %get-tuple-element.272, f32[256,256]{1,0:T(8,128)S(1)} %bitcast_add_fusion.2, s32[]{:T(128)S(6)} %select_n.121, s32[]{:T(128)S(6)} %select_n.122) | dynamic-update-slice | bytes 524292 | tf_op jit(solution)/shard_map/while/body/eval_jaxpr/dynamic_update_slice | solution.py:17
  67.5 0.6 dynamic_slice.75
  68.9 2.1 dynamic_update_slice.11
  76.1 0.6 dynamic_slice.75
  77.5 2.6 dynamic_update_slice.11
  85.2 0.6 dynamic_slice.75
  86.6 3.3 %dynamic_update_slice.11 = f32[512,512]{1,0:T(8,128)S(1)} dynamic-update-slice(f32[512,512]{1,0:T(8,128)S(1)} %get-tuple-element.272, f32[256,256]{1,0:T(8,128)S(1)} %bitcast_add_fusion.2, s32[]{:T(128)S(6)} %select_n.121, s32[]{:T(128)S(6)} %select_n.122) | dynamic-update-slice | bytes 524292 | tf_op jit(solution)/shard_map/while/body/eval_jaxpr/dynamic_update_slice | solution.py:17
  94.9 0.6 dynamic_slice.75
  96.3 3.0 dynamic_update_slice.11
  104.4 0.6 dynamic_slice.75
  105.8 3.9 %dynamic_update_slice.11 = f32[512,512]{1,0:T(8,128)S(1)} dynamic-update-slice(f32[512,512]{1,0:T(8,128)S(1)} %get-tuple-element.272, f32[256,256]{1,0:T(8,128)S(1)} %bitcast_add_fusion.2, s32[]{:T(128)S(6)} %select_n.121, s32[]{:T(128)S(6)} %select_n.122) | dynamic-update-slice | bytes 524292 | tf_op jit(solution)/shard_map/while/body/eval_jaxpr/dynamic_update_slice | solution.py:17
  114.8 0.6 dynamic_slice.75
  116.2 4.7 %dynamic_update_slice.11 = f32[512,512]{1,0:T(8,128)S(1)} dynamic-update-slice(f32[512,512]{1,0:T(8,128)S(1)} %get-tuple-element.272, f32[256,256]{1,0:T(8,128)S(1)} %bitcast_add_fusion.2, s32[]{:T(128)S(6)} %select_n.121, s32[]{:T(128)S(6)} %select_n.122) | dynamic-update-slice | bytes 524292 | tf_op jit(solution)/shard_map/while/body/eval_jaxpr/dynamic_update_slice | solution.py:17
  126.0 0.6 dynamic_slice.75
  127.4 3.9 %dynamic_update_slice.11 = f32[512,512]{1,0:T(8,128)S(1)} dynamic-update-slice(f32[512,512]{1,0:T(8,128)S(1)} %get-tuple-element.272, f32[256,256]{1,0:T(8,128)S(1)} %bitcast_add_fusion.2, s32[]{:T(128)S(6)} %select_n.121, s32[]{:T(128)S(6)} %select_n.122) | dynamic-update-slice | bytes 524292 | tf_op jit(solution)/shard_map/while/body/eval_jaxpr/dynamic_update_slice | solution.py:17
  136.4 0.6 dynamic_slice.75
  137.8 2.6 dynamic_update_slice.11
  145.4 0.6 dynamic_slice.75
  146.8 3.9 %dynamic_update_slice.11 = f32[512,512]{1,0:T(8,128)S(1)} dynamic-update-slice(f32[512,512]{1,0:T(8,128)S(1)} %get-tuple-element.272, f32[256,256]{1,0:T(8,128)S(1)} %bitcast_add_fusion.2, s32[]{:T(128)S(6)} %select_n.121, s32[]{:T(128)S(6)} %select_n.122) | dynamic-update-slice | bytes 524292 | tf_op jit(solution)/shard_map/while/body/eval_jaxpr/dynamic_update_slice | solution.py:17
  155.8 0.6 dynamic_slice.75
  157.2 3.9 %dynamic_update_slice.11 = f32[512,512]{1,0:T(8,128)S(1)} dynamic-update-slice(f32[512,512]{1,0:T(8,128)S(1)} %get-tuple-element.272, f32[256,256]{1,0:T(8,128)S(1)} %bitcast_add_fusion.2, s32[]{:T(128)S(6)} %select_n.121, s32[]{:T(128)S(6)} %select_n.122) | dynamic-update-slice | bytes 524292 | tf_op jit(solution)/shard_map/while/body/eval_jaxpr/dynamic_update_slice | solution.py:17
  166.2 0.6 dynamic_slice.75
  167.6 3.3 %dynamic_update_slice.11 = f32[512,512]{1,0:T(8,128)S(1)} dynamic-update-slice(f32[512,512]{1,0:T(8,128)S(1)} %get-tuple-element.272, f32[256,256]{1,0:T(8,128)S(1)} %bitcast_add_fusion.2, s32[]{:T(128)S(6)} %select_n.121, s32[]{:T(128)S(6)} %select_n.122) | dynamic-update-slice | bytes 524292 | tf_op jit(solution)/shard_map/while/body/eval_jaxpr/dynamic_update_slice | solution.py:17
  176.0 0.6 dynamic_slice.75
  177.4 3.0 dynamic_update_slice.11
  185.5 0.6 dynamic_slice.75
  186.9 3.9 %dynamic_update_slice.11 = f32[512,512]{1,0:T(8,128)S(1)} dynamic-update-slice(f32[512,512]{1,0:T(8,128)S(1)} %get-tuple-element.272, f32[256,256]{1,0:T(8,128)S(1)} %bitcast_add_fusion.2, s32[]{:T(128)S(6)} %select_n.121, s32[]{:T(128)S(6)} %select_n.122) | dynamic-update-slice | bytes 524292 | tf_op jit(solution)/shard_map/while/body/eval_jaxpr/dynamic_update_slice | solution.py:17
  190.8 1.0 broadcast_select_fusion.1
  191.8 0.9 broadcast_select_fusion.2
  192.8 51.9 %all-reduce.6.cloned.1.call-done = (bf16[512,512]{1,0:T(8,128)(2,1)}, bf16[512,512]{1,0:T(8,128)(2,1)}) async-done(((bf16[512,512]{1,0:T(8,128)(2,1)}, bf16[512,512]{1,0:T(8,128)(2,1)}), (bf16[512,512]{1,0:T(8,128)(2,1)}, bf16[512,512]{1,0:T(8,128)(2,1)})) %all-reduce.6.cloned.1.call-update) | async-done | bytes 1048592 | tf_op jit(solution)/shard_map/psum | solution.py:11
  244.7 1.1 constant_dynamic-update-slice_fusion.1
  245.8 1.1 constant_dynamic-update-slice_fusion
  246.9 1.0 broadcast_select_fusion
  248.0 59.5 %all-reduce.4.cloned.1.call-done = bf16[1024,512]{1,0:T(8,128)(2,1)} async-done(((bf16[1024,512]{1,0:T(8,128)(2,1)}), bf16[1024,512]{1,0:T(8,128)(2,1)}) %all-reduce.4.cloned.1.call-update) | async-done | bytes 1048592 | tf_op jit(solution)/shard_map/psum | solution.py:11
  307.5 3.1 convolution_subtract_fusion
  (69 shorter events, 23.4 us)
Async XLA Ops:
  17.8 7.2 %copy-start.1 = (s32[4,4,2]{1,2,0:T(2,128)S(1)}, s32[4,4,2]{1,2,0:T(2,128)}, u32[]{:S(2)}) copy-start(s32[4,4,2]{1,2,0:T(2,128)} %param.13) | copy-start | bytes 388
  19.7 13.2 %all-to-all-start = ((bf16[4,1,256,256]{3,2,1,0:T(8,128)(2,1)}), bf16[4,1,256,256]{3,2,1,0:T(8,128)(2,1)S(1)}, u32[]{:S(2)}, u32[]{:S(2)}) async-start(bf16[4,1,256,256]{3,2,1,0:T(8,128)(2,1)} %bitcast.48), calls=%async_computation | async-start | bytes 1048576 | tf_op jit(solution)/shard_map/all_to_all | solution.py:58
  24.9 219.8 %all-reduce.6.cloned.1.call-start = ((), (), s32[]{:S(2)}) async-start(), calls=%async_computation.2 | async-start | bytes 2097152 | tf_op jit(solution)/shard_map/psum | solution.py:11
  33.1 157.7 %copy-start = (f32[512,512]{1,0:T(8,128)S(1)}, f32[512,512]{1,0:T(8,128)}, u32[]{:S(2)}) copy-start(f32[512,512]{1,0:T(8,128)} %param.14) | copy-start | bytes 3145732
  192.7 114.7 %all-reduce.4.cloned.1.call-start = ((), (), s32[]{:S(2)}) async-start(), calls=%async_computation.1 | async-start | bytes 2097152 | tf_op jit(solution)/shard_map/psum | solution.py:11
  245.8 61.6 %copy-start.2 = (f32[1024]{0:T(1024)S(1)}, f32[1024]{0:T(1024)}, u32[]{:S(2)}) copy-start(f32[1024]{0:T(1024)} %param.15) | copy-start | bytes 12292
Sparse Core Ops, SparseCore 0:
  192.8 51.8 all-reduce.5
  248.1 59.2 all-reduce.3
where the time goes:
time: 319 us; the launch traced here: 317 us
  waiting for transfers between devices  119 us (37%)
  local copies, waits for them, and re-layouts  86.3 us (27%)
  loops' own time  73.4 us (23%)
  between operations  13.5 us (4%)
  matrix products  11.2 us (4%)
  other arithmetic  8.52 us (3%)
  starting transfers between devices  5.23 us (2%)
    psum x2, waiting for transfers between devices, spread(): return lax.psum(kept, axis)  111 us
    another operation x1, loops' own time, body(): schur_sum = lax.fori_loop(0, targets.shape[0], one_slot, zero_sum)  73.4 us
    dynamic_update_slice x16, local copies, waits for them, and re-layouts, place_tile(): lax.dynamic_update_slice(schur_sum, current + weight * tile_value.astype(...  53.6 us
    dynamic_slice x16, local copies, waits for them, and re-layouts, one_slot(): weight = (targets[position] == my_row).astype(jnp.float32)  9.42 us
    dynamic_slice x16, local copies, waits for them, and re-layouts, one_slot(): col_starts[position]  9.41 us
    dynamic_slice x16, local copies, waits for them, and re-layouts, one_slot(): row_starts[position]  9.39 us
    all_to_all x1, waiting for transfers between devices, body(): lax.all_to_all(send_slots, 'row', split_axis=0, concat_axis=0, tiled=True)  7.82 us
    dot_general x1, matrix products, body(): jnp.einsum('sji,sjk->sik', masked, solved, preferred_element_type=jnp.flo...  7.49 us
  transfers between devices with their start and end apart: 3, of which 3 were waited for; matrix products, arithmetic and copies ran while one was open for 0% of the time, Pallas kernels for 0%

commit v1 on v0

--- a/solution.py
+++ b/solution.py
@@ -8,7 +8,7 @@
 
 def spread(value, axis, source):
     kept = jnp.where(lax.axis_index(axis) == source, value, 0).astype(value.dtype)
-    return lax.psum(kept, axis)
+    return jnp.sum(lax.all_gather(kept, axis), axis=0)
 
 
 def place_tile(schur_sum, tile_value, weight, row_start, col_start):

time: 319 us -> 367 us (1.15)
  waiting for transfers between devices: 119 us -> 159 us
  other arithmetic: 8.52 us -> 20.1 us
    all_gather x0 -> x3, waiting for transfers between devices: none -> 151 us  [spread(): return jnp.sum(lax.all_gather(kept, axis), axis=0)]
    psum x2 -> x0, waiting for transfers between devices: 111 us -> none  [spread(): return lax.psum(kept, axis)]
    reduce_sum x0 -> x3, other arithmetic: none -> 10.3 us  [spread(): return jnp.sum(lax.all_gather(kept, axis), axis=0)]
  transfers between devices with their start and end apart: 3 -> 4, of which waited for: 3 -> 4; matrix products, arithmetic and copies ran while one was open for 0% -> 1% of each run, Pallas kernels for 0% -> 0%
where the time goes in v1:
time: 367 us; the launch traced here: 366 us
  waiting for transfers between devices  159 us (43%)
  local copies, waits for them, and re-layouts  84.1 us (23%)
  loops' own time  73.4 us (20%)
  other arithmetic  20.1 us (5%)
  between operations  13.2 us (4%)
  matrix products  11.2 us (3%)
  starting transfers between devices  5.28 us (1%)
    all_gather x3, waiting for transfers between devices, spread(): return jnp.sum(lax.all_gather(kept, axis), axis=0)  151 us
    another operation x1, loops' own time, body(): schur_sum = lax.fori_loop(0, targets.shape[0], one_slot, zero_sum)  73.4 us
    dynamic_update_slice x16, local copies, waits for them, and re-layouts, place_tile(): lax.dynamic_update_slice(schur_sum, current + weight * tile_value.astype(...  53.6 us
    reduce_sum x3, other arithmetic, spread(): return jnp.sum(lax.all_gather(kept, axis), axis=0)  10.3 us
    dynamic_slice x16, local copies, waits for them, and re-layouts, one_slot(): col_starts[position]  9.42 us
    dynamic_slice x16, local copies, waits for them, and re-layouts, one_slot(): weight = (targets[position] == my_row).astype(jnp.float32)  9.41 us
    dynamic_slice x16, local copies, waits for them, and re-layouts, one_slot(): row_starts[position]  9.38 us
    all_to_all x1, waiting for transfers between devices, body(): lax.all_to_all(send_slots, 'row', split_axis=0, concat_axis=0, tiled=True)  7.82 us
  transfers between devices with their start and end apart: 4, of which 4 were waited for; matrix products, arithmetic and copies ran while one was open for 1% of the time, Pallas kernels for 0%

profile of v1, /device:TPU:0, one launch (start us, length us, event | category | flops | bytes accessed | tf_op | source)
XLA Modules:
  0.0 365.9 jit_solution(6108553858237555099)
XLA Ops:
  6.5 1.0 convert_reduce_fusion
  8.1 1.3 reduce.14
  9.5 0.7 iota_compare_fusion
  10.3 7.5 %fusion.13 = bf16[1,4,256,256]{3,2,1,0:T(8,128)(2,1)S(1)} fusion(bf16[1,4,1024,1024]{3,2,1,0:T(8,128)(2,1)} %param.9, bf16[1,4,1024,256]{3,2,1,0:T(8,128)(2,1)} %param.10, pred[4,1024]{1,0:T(4,128)(4,1)S(1)} %iota_compare_fusion), kind=kOutput, calls=%fused_computation.10 | convolution fusion | flops 2687762432 | bytes 11014144 | tf_op jit(solution)/shard_map/sji,sjk->sik/dot_general | solution.py:34
  18.9 0.9 copy.23
  19.7 5.2 %all-to-all-start = ((bf16[4,1,256,256]{3,2,1,0:T(8,128)(2,1)}), bf16[4,1,256,256]{3,2,1,0:T(8,128)(2,1)S(1)}, u32[]{:S(2)}, u32[]{:S(2)}) async-start(bf16[4,1,256,256]{3,2,1,0:T(8,128)(2,1)} %bitcast.51), calls=%async_computation | async-start | bytes 1048576 | tf_op jit(solution)/shard_map/all_to_all | solution.py:58
  25.1 7.8 %all-to-all-done = bf16[4,1,256,256]{3,2,1,0:T(8,128)(2,1)S(1)} async-done(((bf16[4,1,256,256]{3,2,1,0:T(8,128)(2,1)}), bf16[4,1,256,256]{3,2,1,0:T(8,128)(2,1)S(1)}, u32[]{:S(2)}, u32[]{:S(2)}) %all-to-all-start) | async-done | bytes 524320 | tf_op jit(solution)/shard_map/all_to_all | solution.py:58
  33.1 157.7 %while.15 = (s32[]{:T(128)}, f32[512,512]{1,0:T(8,128)S(1)}, s32[16]{0:T(128)S(1)}, s32[16]{0:T(128)S(1)}, s32[16]{0:T(128)S(1)}, /*index=5*/s32[]{:T(128)}, bf1...) while((s32[]{:T(128)}, f32[512,512]{1,0:T(8,128)S(1)}, ...), condition=%wide.region_2.3_spmd, body=%wide.region_1.2_spmd.sunk | while | flops 196629 | bytes 1180039 | solution.py:66
  35.6 0.6 dynamic_slice.74
  39.6 2.6 dynamic_update_slice.11
  44.7 0.6 dynamic_slice.74
  48.6 2.6 dynamic_update_slice.11
  53.7 0.6 dynamic_slice.74
  57.7 4.7 %dynamic_update_slice.11 = f32[512,512]{1,0:T(8,128)S(1)} dynamic-update-slice(f32[512,512]{1,0:T(8,128)S(1)} %get-tuple-element.270, f32[256,256]{1,0:T(8,128)S(1)} %bitcast_add_fusion.2, s32[]{:T(128)S(6)} %select_n.128, s32[]{:T(128)S(6)} %select_n.129) | dynamic-update-slice | bytes 524292 | tf_op jit(solution)/shard_map/while/body/eval_jaxpr/dynamic_update_slice | solution.py:17
  64.9 0.6 dynamic_slice.74
  68.9 2.1 dynamic_update_slice.11
  73.5 0.6 dynamic_slice.74
  77.5 2.6 dynamic_update_slice.11
  82.6 0.6 dynamic_slice.74
  86.5 3.3 dynamic_update_slice.11
  92.4 0.6 dynamic_slice.74
  96.3 3.0 dynamic_update_slice.11
  101.9 0.6 dynamic_slice.74
  105.8 3.9 %dynamic_update_slice.11 = f32[512,512]{1,0:T(8,128)S(1)} dynamic-update-slice(f32[512,512]{1,0:T(8,128)S(1)} %get-tuple-element.270, f32[256,256]{1,0:T(8,128)S(1)} %bitcast_add_fusion.2, s32[]{:T(128)S(6)} %select_n.128, s32[]{:T(128)S(6)} %select_n.129) | dynamic-update-slice | bytes 524292 | tf_op jit(solution)/shard_map/while/body/eval_jaxpr/dynamic_update_slice | solution.py:17
  112.2 0.6 dynamic_slice.74
  116.2 4.7 %dynamic_update_slice.11 = f32[512,512]{1,0:T(8,128)S(1)} dynamic-update-slice(f32[512,512]{1,0:T(8,128)S(1)} %get-tuple-element.270, f32[256,256]{1,0:T(8,128)S(1)} %bitcast_add_fusion.2, s32[]{:T(128)S(6)} %select_n.128, s32[]{:T(128)S(6)} %select_n.129) | dynamic-update-slice | bytes 524292 | tf_op jit(solution)/shard_map/while/body/eval_jaxpr/dynamic_update_slice | solution.py:17
  123.4 0.6 dynamic_slice.74
  127.4 3.9 %dynamic_update_slice.11 = f32[512,512]{1,0:T(8,128)S(1)} dynamic-update-slice(f32[512,512]{1,0:T(8,128)S(1)} %get-tuple-element.270, f32[256,256]{1,0:T(8,128)S(1)} %bitcast_add_fusion.2, s32[]{:T(128)S(6)} %select_n.128, s32[]{:T(128)S(6)} %select_n.129) | dynamic-update-slice | bytes 524292 | tf_op jit(solution)/shard_map/while/body/eval_jaxpr/dynamic_update_slice | solution.py:17
  133.8 0.6 dynamic_slice.74
  137.8 2.6 dynamic_update_slice.11
  142.9 0.6 dynamic_slice.74
  146.8 3.9 %dynamic_update_slice.11 = f32[512,512]{1,0:T(8,128)S(1)} dynamic-update-slice(f32[512,512]{1,0:T(8,128)S(1)} %get-tuple-element.270, f32[256,256]{1,0:T(8,128)S(1)} %bitcast_add_fusion.2, s32[]{:T(128)S(6)} %select_n.128, s32[]{:T(128)S(6)} %select_n.129) | dynamic-update-slice | bytes 524292 | tf_op jit(solution)/shard_map/while/body/eval_jaxpr/dynamic_update_slice | solution.py:17
  157.2 3.9 %dynamic_update_slice.11 = f32[512,512]{1,0:T(8,128)S(1)} dynamic-update-slice(f32[512,512]{1,0:T(8,128)S(1)} %get-tuple-element.270, f32[256,256]{1,0:T(8,128)S(1)} %bitcast_add_fusion.2, s32[]{:T(128)S(6)} %select_n.128, s32[]{:T(128)S(6)} %select_n.129) | dynamic-update-slice | bytes 524292 | tf_op jit(solution)/shard_map/while/body/eval_jaxpr/dynamic_update_slice | solution.py:17
  167.6 3.3 dynamic_update_slice.11
  173.5 0.6 dynamic_slice.74
  177.4 3.0 dynamic_update_slice.11
  182.9 0.6 dynamic_slice.74
  186.9 3.9 %dynamic_update_slice.11 = f32[512,512]{1,0:T(8,128)S(1)} dynamic-update-slice(f32[512,512]{1,0:T(8,128)S(1)} %get-tuple-element.270, f32[256,256]{1,0:T(8,128)S(1)} %bitcast_add_fusion.2, s32[]{:T(128)S(6)} %select_n.128, s32[]{:T(128)S(6)} %select_n.129) | dynamic-update-slice | bytes 524292 | tf_op jit(solution)/shard_map/while/body/eval_jaxpr/dynamic_update_slice | solution.py:17
  190.8 2.3 broadcast_select_fusion.1
  193.1 0.8 broadcast_select_fusion
  194.0 33.7 %all-gather.8.cloned.1.call-done = bf16[2048,512]{1,0:T(8,128)(2,1)} async-done(((bf16[512,512]{1,0:T(8,128)(2,1)}), bf16[2048,512]{1,0:T(8,128)(2,1)}) %all-gather.8.cloned.1.call-update) | async-done | bytes 2097168 | tf_op jit(solution)/shard_map/all_gather | solution.py:11
  227.8 2.2 reduce_sum.46
  229.9 34.9 %all-gather.10.cloned.1.call-done = bf16[2048,512]{1,0:T(8,128)(2,1)} async-done(((bf16[512,512]{1,0:T(8,128)(2,1)}), bf16[2048,512]{1,0:T(8,128)(2,1)}) %all-gather.10.cloned.1.call-update) | async-done | bytes 2097168 | tf_op jit(solution)/shard_map/all_gather | solution.py:11
  264.8 2.2 reduce_sum.47
  267.0 1.2 maximum_select_fusion
  268.2 82.2 %all-gather.6.cloned.1.call-done = bf16[8,1024,512]{2,1,0:T(8,128)(2,1)} async-done(((bf16[1,1024,512]{2,1,0:T(8,128)(2,1)}), bf16[8,1024,512]{2,1,0:T(8,128)(2,1)}) %all-gather.6.cloned.1.call-update) | async-done | bytes 8388624 | tf_op jit(solution)/shard_map/all_gather | solution.py:11
  350.4 6.0 %reduce_sum.48 = bf16[1024,512]{1,0:T(8,128)(2,1)} reduce(bf16[8,1024,512]{2,1,0:T(8,128)(2,1)} %all-gather.6.cloned.1.call-done, bf16[]{:T(256)} %constant.108.clone.1), dimensions={0}, to_apply=%region_5.6 | reduce | flops 3670016 | bytes 9437186 | tf_op jit(solution)/shard_map/reduce_sum | solution.py:11
  356.3 3.1 convolution_subtract_fusion
  (71 shorter events, 24.6 us)
Async XLA Ops:
  17.8 7.2 %copy-start = (s32[4,4,2]{1,2,0:T(2,128)S(1)}, s32[4,4,2]{1,2,0:T(2,128)}, u32[]{:S(2)}) copy-start(s32[4,4,2]{1,2,0:T(2,128)} %param.13) | copy-start | bytes 388
  19.7 13.2 %all-to-all-start = ((bf16[4,1,256,256]{3,2,1,0:T(8,128)(2,1)}), bf16[4,1,256,256]{3,2,1,0:T(8,128)(2,1)S(1)}, u32[]{:S(2)}, u32[]{:S(2)}) async-start(bf16[4,1,256,256]{3,2,1,0:T(8,128)(2,1)} %bitcast.51), calls=%async_computation | async-start | bytes 1048576 | tf_op jit(solution)/shard_map/all_to_all | solution.py:58
  24.9 202.8 %all-gather.8.cloned.1.call-start = ((), (), s32[]{:S(2)}) async-start(), calls=%async_computation.2 | async-start | bytes 2621440 | tf_op jit(solution)/shard_map/all_gather | solution.py:11
  193.1 71.8 %all-gather.10.cloned.1.call-start = ((), (), s32[]{:S(2)}) async-start(), calls=%async_computation.3 | async-start | bytes 2621440 | tf_op jit(solution)/shard_map/all_gather | solution.py:11
  194.0 156.4 %all-gather.6.cloned.1.call-start = ((), (), s32[]{:S(2)}) async-start(), calls=%async_computation.1 | async-start | bytes 9437184 | tf_op jit(solution)/shard_map/all_gather | solution.py:11
  268.2 88.1 %copy-start.1 = (f32[1024]{0:T(1024)S(1)}, f32[1024]{0:T(1024)}, u32[]{:S(2)}) copy-start(f32[1024]{0:T(1024)} %param.15) | copy-start | bytes 12292
Sparse Core Ops, SparseCore 0:
  193.2 34.5 all-gather.7
  229.6 35.1 all-gather.9
  268.3 82.0 all-gather.5
